TPU v7x, 128 devices: a whole 4x4x4 slice. The times are simulated.
128 devices in a mesh: row: 16 (over x, y), col: 8 (over z, core).
Axes of the slice: x: 4, y: 4, z: 4, core: 2. Of those that a mesh axis runs over, the one named last changes fastest.
Arguments:
- saved_factor: float32 [8192, 8192], P('row', 'col'), may hold values from -1 to 3, as said below
- cotangent: float32 [8192, 8192], P('row', 'col'), may hold values from -6 to 6
Outputs:
- adjoint: float32 [8192, 8192], P('row', 'col')
Inputs may be any that keep to these rules, and one draw needn't show every extreme that they name: `saved_factor`: entry (i, j) is zero where j > i + 8192 - 3 * 512, and 1 or more where j = i + 8192 - 3 * 512.
All inputs are finite; a program needn't handle non-finite values.
Results may differ from a plain program's by a relative error of at most 0.0001.
Values sent between devices are 32-bit elements; how exact they have to be, the bound alone decides.
A program may use at most 128 MiB of HBM per device.

v0:
```python
import jax
import jax.numpy as jnp
from jax import lax
from jax.sharding import PartitionSpec as P

NB = 512
NP = 3


precise = lax.Precision.HIGHEST


def from_root(shard, axis, root):
    mine = lax.axis_index(axis) == root
    return lax.psum(jnp.where(mine, shard, jnp.zeros_like(shard)), axis)


def matmul(left_side, right_side):
    return jnp.dot(left_side, right_side, precision=precise, preferred_element_type=jnp.float32)


def inner_rows(left_side, right_side):
    return lax.dot_general(
        left_side,
        right_side,
        (((0,), (0,)), ((), ())),
        precision=precise,
        preferred_element_type=jnp.float32,
    )


def lower_half(matrix):
    return jnp.tril(matrix) - 0.5 * jnp.diag(jnp.diag(matrix))


def adjoint_of(diag_factor, diag_cot, diag_sum, inverse):
    diag_grad = jnp.tril(diag_cot) - jnp.tril(diag_sum)
    return lower_half(
        matmul(matmul(inverse.T, lower_half(matmul(diag_factor.T, diag_grad))), inverse)
    )


def fetch(saved_factor, cotangent, row_start, col_start, rows_dev, cols_dev, col_count):
    owner_row = row_start // rows_dev
    owner_col = col_start // cols_dev
    row_shift = row_start % rows_dev
    col_shift = col_start % cols_dev
    blocks = jnp.stack(
        [
            saved_factor[row_shift : row_shift + NB, col_shift : col_shift + NB],
            cotangent[row_shift : row_shift + NB, col_shift : col_shift + NB],
        ]
    )
    blocks = from_root(blocks, ("row", "col"), owner_row * col_count + owner_col)
    strip_rows = from_root(saved_factor, "row", owner_row)
    return (blocks, strip_rows)


def shards(saved_factor, cotangent):
    rows_dev, cols_dev = saved_factor.shape
    row_count = lax.axis_size("row")
    col_count = lax.axis_size("col")
    full_order = rows_dev * row_count
    this_row = lax.axis_index("row")
    this_col = lax.axis_index("col")
    row_ids = this_row * rows_dev + jnp.arange(rows_dev, dtype=jnp.int32)
    col_ids = this_col * cols_dev + jnp.arange(cols_dev, dtype=jnp.int32)
    row_starts = [(NP - 1 - number) * NB for number in range(NP)]
    col_starts = [full_order - (number + 1) * NB for number in range(NP)]
    identity = jnp.eye(NB, dtype=saved_factor.dtype)
    running = cotangent
    for number in range(NP):
        row_start = row_starts[number]
        row_end = row_start + NB
        col_start = col_starts[number]
        blocks, strip_rows = fetch(
            saved_factor, cotangent, row_start, col_start, rows_dev, cols_dev, col_count
        )
        owner_row = row_start // rows_dev
        owner_col = col_start // cols_dev
        row_shift = row_start % rows_dev
        col_shift = col_start % cols_dev
        diag_factor = blocks[0]
        diag_cot = blocks[1]
        inverse = lax.linalg.triangular_solve(diag_factor, identity, left_side=True, lower=True)
        below_mask = (row_ids >= row_end)[:, None]
        left_mask = (col_ids < col_start)[None, :]
        owns_col = this_col == owner_col
        owns_row = this_row == owner_row
        panel_cot = jnp.where(below_mask, running[:, col_shift : col_shift + NB], 0.0)
        panel_factor = jnp.where(below_mask, saved_factor[:, col_shift : col_shift + NB], 0.0)
        arrived = from_root(jnp.stack([matmul(panel_cot, inverse), panel_factor]), "col", owner_col)
        solved = arrived[0]
        below_factor = arrived[1]
        running = running.at[:, col_shift : col_shift + NB].set(
            jnp.where(owns_col & below_mask, solved, running[:, col_shift : col_shift + NB])
        )
        left_strip = jnp.where(left_mask, strip_rows, 0.0)
        running = running - matmul(solved, left_strip)
        left_block = jnp.where(below_mask & left_mask, saved_factor, 0.0)
        strip_part = inner_rows(solved, left_block)
        diag_part = inner_rows(solved, below_factor)
        old_strip = running
        share_rows = NB // row_count
        term = jnp.where(owns_row, old_strip, 0.0) - strip_part
        strip_share = lax.psum_scatter(term, "row", scatter_dimension=0, tiled=True)
        diag_sum = lax.psum(diag_part, "row")
        diag_adj = adjoint_of(diag_factor, diag_cot, diag_sum, inverse)
        sym_rows = lax.dynamic_slice_in_dim(
            diag_adj + diag_adj.T, this_row * share_rows, share_rows, 0
        )
        strip_share = strip_share - matmul(sym_rows, left_strip)
        new_strip = lax.all_gather(strip_share, "row", axis=0, tiled=True)
        running = running.at[row_shift : row_shift + NB, :].set(
            jnp.where(owns_row, new_strip, old_strip)
        )
        running = running.at[row_shift : row_shift + NB, col_shift : col_shift + NB].set(
            jnp.where(
                owns_row & owns_col,
                diag_adj,
                running[row_shift : row_shift + NB, col_shift : col_shift + NB],
            )
        )
    return running


def solution(mesh):
    placed = (P("row", "col"), P("row", "col"))
    return jax.shard_map(
        shards, mesh=mesh, in_specs=placed, out_specs=P("row", "col"), check_vma=False
    )
```

profile of v0, /device:TPU:1, one launch (start us, length us, event | category | flops | bytes accessed | tf_op | source)
XLA Modules:
  0.0 1209.7 jit_solution(10801127162515345611)
XLA Ops:
  19.0 161.7 %all-reduce.18.cloned.1.call-done = (f32[2,512,512]{2,1,0:T(8,128)}, f32[2,512,512]{2,1,0:T(8,128)}, f32[2,512,512]{2,1,0:T(8,128)}) async-done(((f32[2,512,512]{2,1,0:T(8,128)}, f32[2,512,512]{2,1,0:T(8,128)}, f32[2,512,512]{2,1,0:T(8,128)}), (f32[2,512,512]{2,1,0:T(8,128)}, f32[2,512,512]{2,1,0:T(8,128)}, f32[2,512,512]{2,1,0:T(8,128)})) %all-reduce.18.cloned.1.call-update) | async-done | bytes 6291472 | tf_op jit(solution)/shard_map/psum | solution.py:15
  183.1 11.4 while.18
  194.5 39.9 %custom-call.17 = f32[4,128,128]{1,2,0:T(8,128)} custom-call(f32[4,128,128]{2,1,0:T(8,128)S(1)} %get-tuple-element.158), custom_call_target="InvertDiagBlocksLowerTriangular" | custom-call | tf_op jit(solution)/shard_map/triangular_solve/custom-call.1 | solution.py:85
  249.0 59.8 %all-reduce.12.cloned.1.call-done = f32[2,512,512]{2,1,0:T(8,128)} async-done(((f32[2,512,512]{2,1,0:T(8,128)}), f32[2,512,512]{2,1,0:T(8,128)}) %all-reduce.12.cloned.1.call-update) | async-done | bytes 2097168 | tf_op jit(solution)/shard_map/psum | solution.py:15
  316.2 93.7 %all-reduce.24.cloned.1.call-done = (f32[512,1024]{1,0:T(8,128)}, f32[512,512]{1,0:T(8,128)}) async-done(((f32[512,1024]{1,0:T(8,128)}, f32[512,512]{1,0:T(8,128)}), (f32[512,1024]{1,0:T(8,128)}, f32[512,512]{1,0:T(8,128)})) %all-reduce.24.cloned.1.call-update) | async-done | bytes 3145744 | tf_op jit(solution)/shard_map/psum | solution.py:15
  409.9 6.3 fusion.29
  417.6 5.3 select_subtract_fusion.2
  444.7 51.1 %reduce-scatter.4.cloned.1.call-done = f32[32,1024]{1,0:T(8,128)} async-done(((f32[512,1024]{1,0:T(8,128)}), f32[32,1024]{1,0:T(8,128)}) %reduce-scatter.4.cloned.1.call-update) | async-done | bytes 131088 | tf_op jit(solution)/shard_map/reduce_scatter | solution.py:106
  502.1 11.5 while.19
  513.6 39.9 %custom-call.18 = f32[4,128,128]{1,2,0:T(8,128)} custom-call(f32[4,128,128]{2,1,0:T(8,128)S(1)} %get-tuple-element.159), custom_call_target="InvertDiagBlocksLowerTriangular" | custom-call | tf_op jit(solution)/shard_map/triangular_solve/custom-call.1 | solution.py:85
  569.7 65.2 %all-reduce.14.cloned.1.call-done = f32[2,512,512]{2,1,0:T(8,128)} async-done(((f32[2,512,512]{2,1,0:T(8,128)}), f32[2,512,512]{2,1,0:T(8,128)}) %all-reduce.14.cloned.1.call-update) | async-done | bytes 2097168 | tf_op jit(solution)/shard_map/psum | solution.py:15
  643.5 92.5 %all-reduce.22.cloned.1.call-done = (f32[512,1024]{1,0:T(8,128)}, f32[512,512]{1,0:T(8,128)}) async-done(((f32[512,1024]{1,0:T(8,128)}, f32[512,512]{1,0:T(8,128)}), (f32[512,1024]{1,0:T(8,128)}, f32[512,512]{1,0:T(8,128)})) %all-reduce.22.cloned.1.call-update) | async-done | bytes 3145744 | tf_op jit(solution)/shard_map/psum | solution.py:15
  736.0 6.3 fusion.32
  743.7 5.2 select_subtract_fusion.1
  769.7 52.2 %reduce-scatter.6.cloned.1.call-done = f32[32,1024]{1,0:T(8,128)} async-done(((f32[512,1024]{1,0:T(8,128)}), f32[32,1024]{1,0:T(8,128)}) %reduce-scatter.6.cloned.1.call-update) | async-done | bytes 131088 | tf_op jit(solution)/shard_map/reduce_scatter | solution.py:106
  828.5 11.5 while.20
  840.0 39.9 %custom-call.19 = f32[4,128,128]{1,2,0:T(8,128)} custom-call(f32[4,128,128]{2,1,0:T(8,128)S(1)} %get-tuple-element.160), custom_call_target="InvertDiagBlocksLowerTriangular" | custom-call | tf_op jit(solution)/shard_map/triangular_solve/custom-call.1 | solution.py:85
  896.9 65.2 %all-reduce.16.cloned.1.call-done = f32[2,512,512]{2,1,0:T(8,128)} async-done(((f32[2,512,512]{2,1,0:T(8,128)}), f32[2,512,512]{2,1,0:T(8,128)}) %all-reduce.16.cloned.1.call-update) | async-done | bytes 2097168 | tf_op jit(solution)/shard_map/psum | solution.py:15
  969.4 93.8 %all-reduce.20.cloned.1.call-done = (f32[512,1024]{1,0:T(8,128)}, f32[512,512]{1,0:T(8,128)}) async-done(((f32[512,1024]{1,0:T(8,128)}, f32[512,512]{1,0:T(8,128)}), (f32[512,1024]{1,0:T(8,128)}, f32[512,512]{1,0:T(8,128)})) %all-reduce.20.cloned.1.call-update) | async-done | bytes 3145744 | tf_op jit(solution)/shard_map/psum | solution.py:15
  1063.1 6.3 fusion.35
  1070.8 5.2 select_subtract_fusion
  1089.2 4.5 gather_fusion.5
  1094.2 54.8 %reduce-scatter.8.cloned.1.call-done = f32[32,1024]{1,0:T(8,128)} async-done(((f32[512,1024]{1,0:T(8,128)}), f32[32,1024]{1,0:T(8,128)}) %reduce-scatter.8.cloned.1.call-update) | async-done | bytes 131088 | tf_op jit(solution)/shard_map/reduce_scatter | solution.py:106
  1152.7 44.4 %all-gather.8.cloned.1.call-done = f32[512,1024]{1,0:T(8,128)} async-done(((f32[32,1024]{1,0:T(8,128)}), f32[512,1024]{1,0:T(8,128)}) %all-gather.8.cloned.1.call-update) | async-done | bytes 2097168 | tf_op jit(solution)/shard_map/all_gather | solution.py:113
  (238 shorter events, 201.7 us)
Async XLA Ops:
  6.5 174.2 %all-reduce.18.cloned.1.call-start = ((), (), s32[]{:S(2)}) async-start(), calls=%async_computation.12 | async-start | bytes 12582912 | tf_op jit(solution)/shard_map/psum | solution.py:15
  18.8 290.1 %all-reduce.12.cloned.1.call-start = ((), (), s32[]{:S(2)}) async-start(), calls=%async_computation.3 | async-start | bytes 4194304 | tf_op jit(solution)/shard_map/psum | solution.py:15
  19.0 221.3 %copy-start.7 = (f32[512,512]{1,0:T(8,128)}, f32[512,512]{1,0:T(8,128)S(1)}, u32[]{:S(2)}) copy-start(f32[512,512]{1,0:T(8,128)S(1)} %fusion.110) | copy-start | bytes 3145732
  234.4 5.4 copy-start.41
  236.9 5.4 copy-start.1
  238.4 5.9 copy-start.16
  245.9 164.0 %all-reduce.24.cloned.1.call-start = ((), (), s32[]{:S(2)}) async-start(), calls=%async_computation.15 | async-start | bytes 6291456 | tf_op jit(solution)/shard_map/psum | solution.py:15
  313.2 182.6 %reduce-scatter.4.cloned.1.call-start = ((), (), s32[]{:S(2)}) async-start(), calls=%async_computation.4 | async-start | bytes 2228224 | tf_op jit(solution)/shard_map/reduce_scatter | solution.py:106
  409.9 7.7 copy-start.10
  422.9 139.5 %all-gather.4.cloned.1.call-start = ((), (), s32[]{:S(2)}) async-start(), calls=%async_computation.5 | async-start | bytes 2228224 | tf_op jit(solution)/shard_map/all_gather | solution.py:113
  499.6 135.3 %all-reduce.14.cloned.1.call-start = ((), (), s32[]{:S(2)}) async-start(), calls=%async_computation.6 | async-start | bytes 4194304 | tf_op jit(solution)/shard_map/psum | solution.py:15
  553.6 5.6 copy-start.42
  569.7 166.4 %all-reduce.22.cloned.1.call-start = ((), (), s32[]{:S(2)}) async-start(), calls=%async_computation.14 | async-start | bytes 6291456 | tf_op jit(solution)/shard_map/psum | solution.py:15
  639.3 182.6 %reduce-scatter.6.cloned.1.call-start = ((), (), s32[]{:S(2)}) async-start(), calls=%async_computation.7 | async-start | bytes 2228224 | tf_op jit(solution)/shard_map/reduce_scatter | solution.py:106
  736.0 7.7 copy-start.12
  749.0 139.8 %all-gather.6.cloned.1.call-start = ((), (), s32[]{:S(2)}) async-start(), calls=%async_computation.8 | async-start | bytes 2228224 | tf_op jit(solution)/shard_map/all_gather | solution.py:113
  825.6 136.4 %all-reduce.16.cloned.1.call-start = ((), (), s32[]{:S(2)}) async-start(), calls=%async_computation.9 | async-start | bytes 4194304 | tf_op jit(solution)/shard_map/psum | solution.py:15
  879.9 5.6 copy-start.40
  896.8 166.3 %all-reduce.20.cloned.1.call-start = ((), (), s32[]{:S(2)}) async-start(), calls=%async_computation.13 | async-start | bytes 6291456 | tf_op jit(solution)/shard_map/psum | solution.py:15
  966.4 182.6 %reduce-scatter.8.cloned.1.call-start = ((), (), s32[]{:S(2)}) async-start(), calls=%async_computation.10 | async-start | bytes 2228224 | tf_op jit(solution)/shard_map/reduce_scatter | solution.py:106
  1063.1 7.6 copy-start.11
  1076.1 121.0 %all-gather.8.cloned.1.call-start = ((), (), s32[]{:S(2)}) async-start(), calls=%async_computation.11 | async-start | bytes 2228224 | tf_op jit(solution)/shard_map/all_gather | solution.py:113
  1080.7 4.6 copy-start.20
  1080.7 4.6 copy-start.29
  (32 other events, 80.1 us)
Sparse Core Ops, SparseCore 0:
  18.9 161.7 all-reduce.17
  246.0 62.7 all-reduce.11
  313.4 96.5 all-reduce.23
  423.0 72.7 reduce-scatter.3
  499.7 44.9 all-gather.3
  569.8 65.0 all-reduce.13
  639.5 96.5 all-reduce.21
  749.1 72.7 reduce-scatter.5
  825.7 44.6 all-gather.5
  896.9 65.0 all-reduce.15
  966.6 96.5 all-reduce.19
  1076.2 72.8 reduce-scatter.7
  1152.8 44.2 all-gather.7
where the time goes:
time: 1220 us; the launch traced here: 1210 us
  waiting for transfers between devices  835 us (68%)
  other arithmetic  165 us (14%)
  matrix products  115 us (9%)
  local copies, waits for them, and re-layouts  78.1 us (6%)
  between operations  14.5 us (1%)
    psum x7, waiting for transfers between devices, from_root(): return lax.psum(jnp.where(mine, shard, jnp.zeros_like(shard)), axis)  632 us
    reduce_scatter x3, waiting for transfers between devices, shards(): strip_share = lax.psum_scatter(term, 'row', scatter_dimension=0, tiled=True)  158 us
    another operation x7, other arithmetic, shards(): lax.linalg.triangular_solve(diag_factor, identity, left_side=True, lower=...  127 us
    dot_general x18, matrix products, matmul(): jnp.dot(left_side, right_side, precision=precise, preferred_element_type=...  60.5 us
    all_gather x3, waiting for transfers between devices, shards(): new_strip = lax.all_gather(strip_share, 'row', axis=0, tiled=True)  44.4 us
    another operation x40, local copies, waits for them, and re-layouts, shards(): lax.linalg.triangular_solve(diag_factor, identity, left_side=True, lower=...  34.2 us
    dot_general x6, matrix products, inner_rows(): lax.dot_general(left_side, right_side, (((0,), (0,)), ((), ())), precisio...  28.9 us
    gather x6, local copies, waits for them, and re-layouts, lower_half(): return jnp.tril(matrix) - 0.5 * jnp.diag(jnp.diag(matrix))  27.1 us
  transfers between devices with their start and end apart: 13, of which 11 were waited for; matrix products, arithmetic and copies ran while one was open for 16% of the time, Pallas kernels for 0%

commit v1 on v0

v1 whole, which is shorter than its diff:
```python
import jax
import jax.numpy as jnp
from jax import lax
from jax.experimental import pallas as pl
from jax.experimental.pallas import tpu as pltpu
from jax.sharding import PartitionSpec as P

NB = 512
NP = 3
MESH = pl.DeviceIdType.MESH
HI = lax.Precision.HIGHEST
MID = lax.Precision.HIGH
F32 = jnp.float32


def dot(a, b, precision=MID):
    return jnp.dot(a, b, precision=precision, preferred_element_type=F32)


def dot_t(a, b, precision=MID):
    return lax.dot_general(
        a, b, (((0,), (0,)), ((), ())), precision=precision, preferred_element_type=F32
    )


def place():
    row = lax.axis_index("row")
    col = lax.axis_index("col")
    return row // 4, row % 4, col // 2, col % 2


def remote(src, dst, send, recv, x, y, z, core):
    return pltpu.make_async_remote_copy(
        src_ref=src,
        dst_ref=dst,
        send_sem=send,
        recv_sem=recv,
        device_id=(x * 4 + y, z * 2 + core),
        device_id_type=MESH,
    )


def greet(devices):
    barrier = pltpu.get_barrier_semaphore()
    for x, y, z, core in devices:
        pl.semaphore_signal(
            barrier, inc=1, device_id=(x * 4 + y, z * 2 + core), device_id_type=MESH
        )
    pl.semaphore_wait(barrier, len(devices))


def plane_and_peer(x, y, z, core):
    out = []
    for dx in range(4):
        for dy in range(4):
            if dx or dy:
                out.append(((x + dx) % 4, (y + dy) % 4, z, core))
    return out + [(x, y, z, 1 - core)]


def spread_kernel(
    own, cot, strips, d6, d7, half, scat_s, scat_r, ag_s, ag_r, ex_s, ex_r, loc
):
    x, y, z, core = place()
    greet(plane_and_peer(x, y, z, core))
    half_copy = remote(
        cot.at[pl.ds(256 * (1 - core), 256)], half, ex_s.at[0], ex_r.at[0], x, y, z, 1 - core
    )
    half_copy.start()

    for p in range(NP):
        is_root = (x == 0) & (y == p)

        @pl.when(is_root)
        def _():
            here = pltpu.make_async_copy(
                own.at[pl.ds(x, 1), pl.ds(y, 1)],
                strips.at[p, pl.ds(x, 1), pl.ds(y, 1)],
                loc.at[0],
            )
            here.start()
            copies = []
            for d in range(1, 16):
                tx, ty = (x + d // 4) % 4, (y + d % 4) % 4
                copy = remote(
                    own.at[pl.ds(tx, 1), pl.ds(ty, 1)],
                    strips.at[p, pl.ds(tx, 1), pl.ds(ty, 1)],
                    scat_s.at[d],
                    scat_r.at[p],
                    tx, ty, z, core,
                )
                copy.start()
                copies.append(copy)
            here.wait()
            for copy in copies:
                copy.wait_send()

        @pl.when(jnp.logical_not(is_root))
        def _():
            remote(
                own.at[pl.ds(x, 1), pl.ds(y, 1)],
                strips.at[p, pl.ds(x, 1), pl.ds(y, 1)],
                scat_s.at[0],
                scat_r.at[p],
                x, y, z, 1 - core,
            ).wait_recv()

    left, right = pl.ds(0, NB), pl.ds(NB, NB)
    first = []
    for d in range(1, 4):
        tx, ty = (x + d) % 4, (y + d) % 4
        block = strips.at[:, pl.ds(x, 1), pl.ds(y, 1), :, left]
        first.append(remote(block, block, ag_s.at[0, d], ag_r.at[0, d], tx, y, z, core))
        block = strips.at[:, pl.ds(x, 1), pl.ds(y, 1), :, right]
        first.append(remote(block, block, ag_s.at[1, d], ag_r.at[1, d], x, ty, z, core))
    for copy in first:
        copy.start()
    for copy in first:
        copy.wait_recv()
    second = []
    for d in range(1, 4):
        tx, ty = (x + d) % 4, (y + d) % 4
        block = strips.at[:, :, pl.ds(y, 1), :, left]
        second.append(remote(block, block, ag_s.at[2, d], ag_r.at[2, d], x, ty, z, core))
        block = strips.at[:, pl.ds(x, 1), :, :, right]
        second.append(remote(block, block, ag_s.at[3, d], ag_r.at[3, d], tx, y, z, core))
    for copy in second:
        copy.start()
    for copy in second:
        copy.wait_recv()

    low = strips.at[:, :, :, :, right]
    high = strips
    send_low = remote(low, d6, ex_s.at[1], ex_r.at[1], x, y, z, 1 - core)
    send_high = remote(high, d7, ex_s.at[2], ex_r.at[2], x, y, z, 1 - core)

    @pl.when(core == 0)
    def _():
        send_low.start()
        here = pltpu.make_async_copy(low, d6, loc.at[1])
        here.start()
        here.wait()
        send_high.wait_recv()
        send_low.wait_send()

    @pl.when(core == 1)
    def _():
        send_high.start()
        here = pltpu.make_async_copy(high, d7, loc.at[1])
        here.start()
        here.wait()
        send_low.wait_recv()
        send_high.wait_send()

    for copy in first + second:
        copy.wait_send()
    half_copy.wait()


def spread(factor, cot):
    own = factor.reshape(4, 4, 32, 1024)
    vm = pl.BlockSpec(memory_space=pltpu.VMEM)
    dma = pltpu.SemaphoreType.DMA
    return pl.pallas_call(
        spread_kernel,
        out_shape=(
            jax.ShapeDtypeStruct((3, 4, 4, 32, 1024), F32),
            jax.ShapeDtypeStruct((3, 4, 4, 32, 512), F32),
            jax.ShapeDtypeStruct((3, 4, 4, 32, 1024), F32),
            jax.ShapeDtypeStruct((256, 1024), F32),
        ),
        in_specs=[vm, pl.BlockSpec(memory_space=pl.ANY)],
        out_specs=(vm, vm, vm, vm),
        scratch_shapes=[
            dma((16,)), dma((3,)), dma((4, 4)), dma((4, 4)), dma((3,)), dma((3,)), dma((2,)),
        ],
        compiler_params=pltpu.CompilerParams(
            collective_id=0, has_side_effects=True, vmem_limit_bytes=48 << 20
        ),
    )(own, cot)


CH = 4
CR = 128 // CH


def along_kernel(src, out, ring_s, ring_r, peer_s, peer_r):
    x, y, z, core = place()
    up, down = (z + 1) % 4, (z + 3) % 4
    greet([(x, y, up, core), (x, y, down, core), (x, y, z, 1 - core)])
    positions = (up, 3 - z)
    targets = (up, down)

    @pl.when(z == 3)
    def _():
        out[pl.ds(core, 1)] = src[...]

    def chunk(owner, way, step):
        return out.at[pl.ds(owner, 1), way, step]

    for step in range(CH):
        for way in range(2):
            pos, target = positions[way], targets[way]
            mine = chunk(core, way, step)
            send = remote(
                mine, mine, ring_s.at[way, step], ring_r.at[way, step], x, y, target, core
            )

            @pl.when(pos > 0)
            def _():
                send.wait_recv()

            @pl.when((z == 3) & (pos < 3))
            def _():
                remote(
                    src.at[:, way, step], mine,
                    ring_s.at[way, step], ring_r.at[way, step], x, y, target, core,
                ).start()

            @pl.when((z != 3) & (pos < 3))
            def _():
                send.start()

            @pl.when(z == 3)
            def _():
                remote(
                    src.at[:, way, step], mine,
                    peer_s.at[way, step], peer_r.at[way, step], x, y, z, 1 - core,
                ).start()

            @pl.when(z != 3)
            def _():
                remote(
                    mine, mine,
                    peer_s.at[way, step], peer_r.at[way, step], x, y, z, 1 - core,
                ).start()

    for step in range(CH):
        for way in range(2):
            pos, target = positions[way], targets[way]
            mine, other = chunk(core, way, step), chunk(1 - core, way, step)
            remote(
                mine, other, peer_s.at[way, step], peer_r.at[way, step], x, y, z, 1 - core
            ).wait()

            @pl.when(pos < 3)
            def _():
                remote(
                    mine, mine, ring_s.at[way, step], ring_r.at[way, step], x, y, target, core
                ).wait_send()


def along(half, collective_id):
    vm = pl.BlockSpec(memory_space=pltpu.VMEM)
    dma = pltpu.SemaphoreType.DMA
    out = pl.pallas_call(
        along_kernel,
        out_shape=jax.ShapeDtypeStruct((2, 2, CH, CR, 1536), F32),
        in_specs=[vm],
        out_specs=vm,
        scratch_shapes=[dma((2, CH)), dma((2, CH)), dma((2, CH)), dma((2, CH))],
        compiler_params=pltpu.CompilerParams(
            collective_id=collective_id, has_side_effects=True, vmem_limit_bytes=16 << 20
        ),
    )(half.reshape(1, 2, CH, CR, 1536))
    return out.reshape(512, 1536)


def gather_kernel(
    part, total, t6, t7, r1a, r1b, a1a, a1b, r2, a2,
    one_s, one_r, two_s, two_r, g_s, g_r, ex_s, ex_r, loc,
):
    x, y, z, core = place()
    greet(plane_and_peer(x, y, z, core))
    left, right = pl.ds(0, NB), pl.ds(NB, NB)
    cols = (left, right)
    one, two = [], []
    for d in range(1, 4):
        tx, ty = (x + d) % 4, (y + d) % 4
        one.append((
            remote(
                part.at[:, pl.ds(tx, 1), :, :, left], r1a.at[d - 1],
                one_s.at[0, d], one_r.at[0, d], tx, y, z, core,
            ),
            remote(
                part.at[:, :, pl.ds(ty, 1), :, right], r1b.at[d - 1],
                one_s.at[1, d], one_r.at[1, d], x, ty, z, core,
            ),
        ))
        two.append((
            remote(
                a1a.at[:, :, pl.ds(ty, 1)], r2.at[0, d - 1],
                two_s.at[0, d], two_r.at[0, d], x, ty, z, core,
            ),
            remote(
                a1b.at[:, pl.ds(tx, 1)], r2.at[1, d - 1],
                two_s.at[1, d], two_r.at[1, d], tx, y, z, core,
            ),
        ))
    for pair in one:
        for copy in pair:
            copy.start()
    for pair in one:
        pair[0].wait_recv()
    a1a[...] = (part[:, pl.ds(x, 1), :, :, left] + r1a[0]) + (r1a[1] + r1a[2])
    for pair in two:
        pair[0].start()
    for pair in one:
        pair[1].wait_recv()
    a1b[...] = (part[:, :, pl.ds(y, 1), :, right] + r1b[0]) + (r1b[1] + r1b[2])
    for pair in two:
        pair[1].start()
    for pair in two:
        pair[0].wait_recv()
    a2[0] = (a1a[:, :, pl.ds(y, 1)] + r2[0, 0]) + (r2[0, 1] + r2[0, 2])
    for pair in two:
        pair[1].wait_recv()
    a2[1] = (a1b[:, pl.ds(x, 1)] + r2[1, 0]) + (r2[1, 1] + r2[1, 2])

    def wanted(q, root, half):
        if q == root:
            return None
        if half == 0:
            if q == 0:
                return False
            return (z == 3) & (core == 1)
        if q == 2:
            return z == 3
        return (z == 3) & (core == 0)

    def under(flag, other, body):
        if flag is None:
            pl.when(other)(body)
        else:
            pl.when(flag & other)(body)

    for root in range(NP):
        at_root = (x == 0) & (y == root)
        for q in range(NP):
            for h in range(2):
                flag = wanted(q, root, h)
                if flag is False:
                    continue
                slot = total.at[q, pl.ds(x, 1), pl.ds(y, 1), :, cols[h]]

                def send():
                    remote(
                        a2.at[h, q], slot, g_s.at[root, q, h], g_r.at[q, h, x * 4 + y],
                        0, root, z, core,
                    ).start()

                def keep():
                    pltpu.make_async_copy(a2.at[h, q], slot, g_s.at[root, q, h]).start()

                under(flag, jnp.logical_not(at_root), send)
                under(flag, at_root, keep)
    for root in range(NP):
        at_root = (x == 0) & (y == root)
        for q in range(NP):
            for h in range(2):
                flag = wanted(q, root, h)
                if flag is False:
                    continue

                def sent():
                    slot = total.at[q, pl.ds(x, 1), pl.ds(y, 1), :, cols[h]]
                    remote(
                        a2.at[h, q], slot, g_s.at[root, q, h], g_r.at[q, h, x * 4 + y],
                        0, root, z, core,
                    ).wait_send()

                def kept():
                    slot = total.at[q, pl.ds(x, 1), pl.ds(y, 1), :, cols[h]]
                    pltpu.make_async_copy(a2.at[h, q], slot, g_s.at[root, q, h]).wait()
                    for d in range(1, 16):
                        sx, sy = (x + d // 4) % 4, (y + d % 4) % 4
                        slot = total.at[q, pl.ds(sx, 1), pl.ds(sy, 1), :, cols[h]]
                        remote(
                            a2.at[h, q], slot, g_s.at[root, q, h], g_r.at[q, h, sx * 4 + sy],
                            0, root, z, 1 - core,
                        ).wait_recv()

                under(flag, jnp.logical_not(at_root), sent)
                under(flag, at_root, kept)

    top = (x == 0) & (y < NP) & (z == 3)
    low = total.at[:, :, :, :, right]
    high = total.at[pl.ds(1, 2)]
    send_low = remote(low, t6, ex_s.at[0], ex_r.at[0], x, y, z, 1 - core)
    send_high = remote(high, t7, ex_s.at[1], ex_r.at[1], x, y, z, 1 - core)

    @pl.when(top & (core == 0))
    def _():
        send_low.start()
        here = pltpu.make_async_copy(low, t6, loc.at[0])
        here.start()
        here.wait()
        send_high.wait_recv()
        send_low.wait_send()

    @pl.when(top & (core == 1))
    def _():
        send_high.start()
        here = pltpu.make_async_copy(high, t7, loc.at[0])
        here.start()
        here.wait()
        send_low.wait_recv()
        send_high.wait_send()

    for pair in one + two:
        for copy in pair:
            copy.wait_send()


def gather(part):
    vm = pl.BlockSpec(memory_space=pltpu.VMEM)
    dma = pltpu.SemaphoreType.DMA
    return pl.pallas_call(
        gather_kernel,
        out_shape=(
            jax.ShapeDtypeStruct((3, 4, 4, 32, 1024), F32),
            jax.ShapeDtypeStruct((3, 4, 4, 32, 512), F32),
            jax.ShapeDtypeStruct((2, 4, 4, 32, 1024), F32),
        ),
        in_specs=[vm],
        out_specs=(vm, vm, vm),
        scratch_shapes=[
            pltpu.VMEM((3, 3, 1, 4, 32, 512), F32),
            pltpu.VMEM((3, 3, 4, 1, 32, 512), F32),
            pltpu.VMEM((3, 1, 4, 32, 512), F32),
            pltpu.VMEM((3, 4, 1, 32, 512), F32),
            pltpu.VMEM((2, 3, 3, 1, 1, 32, 512), F32),
            pltpu.VMEM((2, 3, 1, 1, 32, 512), F32),
            dma((2, 4)), dma((2, 4)), dma((2, 4)), dma((2, 4)),
            dma((3, 3, 2)), dma((3, 2, 16)), dma((2,)), dma((2,)), dma((1,)),
        ],
        compiler_params=pltpu.CompilerParams(
            collective_id=2, has_side_effects=True, vmem_limit_bytes=48 << 20
        ),
    )(part.reshape(3, 4, 4, 32, 1024))


BS = 128


def invert_kernel(d_ref, o_ref):
    rows = lax.broadcasted_iota(jnp.int32, (BS, BS), 0)
    cols = lax.broadcasted_iota(jnp.int32, (BS, BS), 1)
    diag = rows == cols
    for block in range(NP * (NB // BS)):
        which, at = block // (NB // BS), pl.ds(block % (NB // BS) * BS, BS)
        base = d_ref[which, at, at]
        scale = jnp.sum(jnp.where(diag, base, 0.0), axis=1, keepdims=True)
        o_ref[which, at, at] = jnp.where(diag, 1.0 / scale, 0.0)
    size = 1
    while size < BS:
        pick = (rows // (2 * size) == cols // (2 * size)) & (
            (rows // size) % 2 > (cols // size) % 2
        )
        for block in range(NP * (NB // BS)):
            which, at = block // (NB // BS), pl.ds(block % (NB // BS) * BS, BS)
            have = o_ref[which, at, at]
            below = jnp.where(pick, d_ref[which, at, at], 0.0)
            o_ref[which, at, at] = have - dot(dot(have, below, HI), have, HI)
        size *= 2
    while size < NB:
        for which in range(NP):
            for base in range(0, NB, 2 * size):
                up, down = pl.ds(base, size), pl.ds(base + size, size)
                corner = dot(
                    dot(o_ref[which, down, down], d_ref[which, down, up], HI),
                    o_ref[which, up, up], HI,
                )
                o_ref[which, down, up] = -corner
                o_ref[which, up, down] = jnp.zeros((size, size), F32)
        size *= 2


def invert(blocks):
    vm = pl.BlockSpec(memory_space=pltpu.VMEM)
    return pl.pallas_call(
        invert_kernel,
        out_shape=jax.ShapeDtypeStruct((NP, NB, NB), F32),
        in_specs=[vm],
        out_specs=vm,
        compiler_params=pltpu.CompilerParams(vmem_limit_bytes=16 << 20),
    )(blocks)


def lower_half(matrix):
    rows = lax.broadcasted_iota(jnp.int32, (NB, NB), 0)
    cols = lax.broadcasted_iota(jnp.int32, (NB, NB), 1)
    return jnp.where(rows > cols, matrix, jnp.where(rows == cols, 0.5 * matrix, 0.0))


def adjoint_of(factor, inverse, cot):
    inner = lower_half(dot_t(factor, jnp.tril(cot)))
    return lower_half(dot(dot_t(inverse, inner), inverse))


def chain(l, inv, t):
    a2 = adjoint_of(l[22], inv[2], t[22])
    y2 = a2 + a2.T
    t21 = t[21] - dot(y2, l[21])
    t20 = t[20] - dot(y2, l[20])
    s21 = dot(t21, inv[1])
    t11 = t[11] - dot_t(s21, l[21])
    t10 = t[10] - dot_t(s21, l[20])
    a1 = adjoint_of(l[11], inv[1], t11)
    y1 = a1 + a1.T
    t10 = t10 - dot(y1, l[10])
    t20 = t20 - dot(s21, l[10])
    s20 = dot(t20, inv[0])
    s10 = dot(t10, inv[0])
    t00 = t[0] - dot_t(s20, l[20]) - dot_t(s10, l[10])
    a0 = adjoint_of(l[0], inv[0], t00)
    y0 = a0 + a0.T
    return (a0, a1, a2), (y0, y1, y2), s10, s20, s21


def shards(factor, cot):
    row = lax.axis_index("row")
    col = lax.axis_index("col")
    core = col % 2
    strips, d6, d7, other_half = spread(factor, cot)
    d6 = d6.reshape(3, NB, NB)
    d7 = d7.reshape(3, NB, 1024)
    l = {
        0: d6[0], 10: d6[1], 20: d6[2],
        11: d7[1, :, :NB], 21: d7[2, :, :NB], 22: d7[2, :, NB:],
    }
    inv = invert(jnp.stack([l[0], l[11], l[22]]))
    my_half = lax.dynamic_slice(cot, (core * 256, 0), (256, 1024))
    g6 = jnp.where(core == 0, my_half, other_half)
    g7 = jnp.where(core == 0, other_half, my_half)
    s2 = dot(g7[:, NB:], inv[2])
    s1 = dot(g7[:, :NB] - dot(s2, l[21]), inv[1])
    s0 = dot(g6[:, NB:] - dot(s2, l[20]) - dot(s1, l[10]), inv[0])
    solved = along(jnp.concatenate([s0, s1, s2], axis=1), 1)
    lower_rows = row >= NP
    strips = strips.reshape(3 * NB, 1024)
    part = jnp.where(lower_rows, -dot_t(solved, factor), 0.0).reshape(3, NB, 1024)
    which = lax.broadcasted_iota(jnp.int32, (3, 1, 1), 0)
    part = jnp.where(which == row, cot[None], part)
    total, t6, t7 = gather(part)
    total = total.reshape(3, NB, 1024)
    t6 = t6.reshape(3, NB, NB)
    t7 = t7.reshape(2, NB, 1024)
    t = {
        0: t6[0], 10: t6[1], 20: t6[2],
        11: t7[0, :, :NB], 21: t7[1, :, :NB], 22: t7[1, :, NB:],
    }
    a, sym, s10, s20, s21 = chain(l, inv, t)
    pick = row
    rows0 = jnp.concatenate([sym[0], s10.T, s20.T], axis=1)
    rows1 = jnp.concatenate([s10, sym[1], s21.T], axis=1)
    rows2 = jnp.concatenate([s20, s21, sym[2]], axis=1)
    mixed = jnp.where(pick == 0, rows0, jnp.where(pick == 1, rows1, rows2))
    mixed_half = lax.dynamic_slice(mixed, (core * 256, 0), (256, 1536))
    mixed = along(mixed_half, 3)
    factor_rows = jnp.where(lower_rows, solved, mixed)
    own_total = lax.dynamic_index_in_dim(total, jnp.minimum(row, 2), 0, keepdims=False)
    start = jnp.where(lower_rows, cot, own_total)
    out = start - dot(factor_rows, strips)
    cut = cot[:, :NB], cot[:, NB:]
    last6 = jnp.where(
        lower_rows, solved[:, :NB],
        jnp.where(pick == 0, a[0], jnp.where(pick == 1, s10, s20)),
    )
    left7 = jnp.where(
        lower_rows, solved[:, NB:1024],
        jnp.where(pick == 0, cut[0], jnp.where(pick == 1, a[1], s21)),
    )
    right7 = jnp.where(
        lower_rows, solved[:, 1024:],
        jnp.where(pick == 2, a[2], cut[1]),
    )
    left = jnp.where(col == 7, left7, out[:, :NB])
    right = jnp.where(col == 7, right7, jnp.where(col == 6, last6, out[:, NB:]))
    return jnp.concatenate([left, right], axis=1)


def solution(mesh):
    placed = (P("row", "col"), P("row", "col"))
    return jax.shard_map(
        shards, mesh=mesh, in_specs=placed, out_specs=P("row", "col"), check_vma=False
    )
```

time: 1220 us -> 489 us (0.40)
  the two profiles are of different devices: /device:TPU:1 before, /device:TPU:9 now
where the time goes in v1:
time: 489 us; the launch traced here: 480 us
  Pallas kernels  374 us (76%)
  matrix products  58.7 us (12%)
  local copies, waits for them, and re-layouts  24.5 us (5%)
  other arithmetic  21.5 us (4%)
    pallas_call x2, Pallas kernels, along(): pl.pallas_call(along_kernel, out_shape=jax.ShapeDtypeStruct((2, 2, CH, CR...  183 us
    pallas_call x1, Pallas kernels, spread(): pl.pallas_call(spread_kernel, out_shape=(jax.ShapeDtypeStruct((3, 4, 4, 3...  96.5 us
    pallas_call x1, Pallas kernels, gather(): pl.pallas_call(gather_kernel, out_shape=(jax.ShapeDtypeStruct((3, 4, 4, 3...  82.5 us
    dot_general x17, matrix products, dot(): return jnp.dot(a, b, precision=precision, preferred_element_type=F32)  32.4 us
    dot_general x11, matrix products, dot_t(): lax.dot_general(a, b, (((0,), (0,)), ((), ())), precision=precision, pref...  26.3 us
    pallas_call x1, Pallas kernels, invert(): pl.pallas_call(invert_kernel, out_shape=jax.ShapeDtypeStruct((NP, NB, NB)...  12.1 us
    dot_general x6, local copies, waits for them, and re-layouts, dot(): return jnp.dot(a, b, precision=precision, preferred_element_type=F32)  11.9 us

profile of v1, /device:TPU:9, one launch (start us, length us, event | category | flops | bytes accessed | tf_op | source)
XLA Modules:
  0.0 479.7 jit_solution(6617173045259862466)
XLA Ops:
  3.2 96.5 %shard_map.28 = (f32[3,4,4,32,1024]{4,3,2,1,0:T(8,128)}, f32[3,4,4,32,512]{4,3,2,1,0:T(8,128)}, f32[3,4,4,32,1024]{4,3,2,1,0:T(8,128)}, f32[256,1024]{1,0:T(8,128)S(1)}) custom-call(f32[4,4,32,1024]{3,2,1,0:T(8,128)S(1)} %bitcast.129, f32[512,1024]{1,0:T(8,128)S(1)} %copy-done.2), custom_call_target="tpu_custom_call" | custom-call | tf_op jit(solution)/shard_map/pallas_call | solution.py:164
  99.9 2.6 fusion.62
  105.7 12.1 %shard_map.29 = f32[3,512,512]{2,1,0:T(8,128)S(1)} custom-call(f32[3,512,512]{2,1,0:T(8,128)S(1)} %pad_maximum_fusion.d_ref), custom_call_target="tpu_custom_call" | custom-call | tf_op jit(solution)/shard_map/pallas_call | solution.py:481
  119.2 2.4 convolution_subtract_fusion.10
  125.6 86.9 %shard_map.30 = f32[2,2,4,32,1536]{4,3,2,1,0:T(8,128)S(1)} custom-call(f32[1,2,4,32,1536]{4,3,2,1,0:T(8,128)S(1)} %bitcast.130), custom_call_target="tpu_custom_call" | custom-call | tf_op jit(solution)/shard_map/pallas_call | solution.py:256
  214.2 7.9 %negate_select_fusion = f32[1536,1024]{1,0:T(8,128)S(1)} fusion(f32[512,1536]{1,0:T(8,128)} %bitcast.126, f32[512,1024]{1,0:T(8,128)} %param.2, pred[]{:T(512)S(6)} %ge.20), kind=kOutput, calls=%fused_computation | convolution fusion | flops 4834983936 | bytes 11534337 | tf_op jit(solution)/shard_map/dot_general | solution.py:21
  222.1 3.7 broadcast_select_fusion.part
  225.7 82.5 %shard_map.31 = (f32[3,4,4,32,1024]{4,3,2,1,0:T(8,128)}, f32[3,4,4,32,512]{4,3,2,1,0:T(8,128)S(1)}, f32[2,4,4,32,1024]{4,3,2,1,0:T(8,128)}) custom-call(f32[3,4,4,32,1024]{4,3,2,1,0:T(8,128)} %broadcast_select_fusion.part), custom_call_target="tpu_custom_call" | custom-call | tf_op jit(solution)/shard_map/pallas_call | solution.py:418
  308.3 3.8 fusion.13
  315.1 2.6 copy.4
  319.4 3.0 convolution_subtract_fusion.7
  328.6 2.1 convolution_subtract_fusion.3
  330.7 2.6 fusion.10
  333.3 2.5 fusion.22
  338.9 2.6 copy.6
  343.7 2.3 convolution_subtract_fusion.2
  351.3 2.0 fusion.41
  353.3 2.7 copy.9
  356.0 2.8 fusion.16
  362.9 2.2 fusion.4
  365.2 95.9 %shard_map.32 = f32[2,2,4,32,1536]{4,3,2,1,0:T(8,128)S(1)} custom-call(f32[1,2,4,32,1536]{4,3,2,1,0:T(8,128)S(1)} %bitcast.131), custom_call_target="tpu_custom_call" | custom-call | tf_op jit(solution)/shard_map/pallas_call | solution.py:256
  461.1 2.2 broadcast_select_fusion.1
  463.3 9.5 %fusion = f32[512,1024]{1,0:T(8,128)} fusion(f32[512,1024]{1,0:T(8,128)} %cot.1, f32[3,512,1024]{2,1,0:T(8,128)} %bitcast.160, s32[]{:T(128)S(6)} %select_n.227, f32[512,1536]{1,0:T(8,128)} %bitcast.144, f32[1536,1024]{1,0:T(8,128)} %bitcast.153, pred[]{:T(512)S(6)} %ge.20), kind=kOutput, calls=%fused_computation.14 | convolution fusion | flops 4832886784 | bytes 15728645 | tf_op jit(solution)/shard_map/dot_general | solution.py:17
  472.8 5.0 %slice_select_fusion.3 = (f32[512,512]{1,0:T(8,128)S(1)}, f32[512,512]{1,0:T(8,128)S(1)}) fusion(f32[512,1024]{1,0:T(8,128)} %fusion, f32[512,1536]{1,0:T(8,128)S(1)} %bitcast.127, f32[512,512]{1,0:T(8,128)} %copy.7, f32[512,1024]{1,0:T(8,128)} %cot.1, f32[512,512]{1,0:T(8,128)} %copy.6, pred[]{:T(512)S(6)} %eq.67, pred[]{:T(512)S(6)} %eq.66, pred[]{:T(512)S(6)} %ge.20, ...), kind=kLoop, calls=%fused_computation.42 | loop fusion | flops 5767168 | bytes 15728646 | tf_op jit(solution)/shard_map/jit(_where)/select_n | solution.py:578
  (88 shorter events, 40.4 us)
Async XLA Ops:
  99.7 2.8 copy-start.7
  99.7 3.3 copy-start.28
  99.9 17.9 %copy-start.25 = (f32[256,1024]{1,0:T(8,128)}, f32[256,1024]{1,0:T(8,128)S(1)}, u32[]{:S(2)}) copy-start(f32[256,1024]{1,0:T(8,128)S(1)} %dynamic-slice_select_fusion) | copy-start | bytes 3145732
  119.2 2.4 copy-start.24
  119.2 2.4 copy-start.26
  121.7 2.6 copy-start.11
  214.2 7.9 %copy-start.3 = (f32[512,1024]{1,0:T(8,128)S(1)}, f32[512,1024]{1,0:T(8,128)}, u32[]{:S(2)}) copy-start(f32[512,1024]{1,0:T(8,128)} %cot.1) | copy-start | bytes 6291460
  308.3 4.9 %copy-start.5 = (f32[3,4,4,32,512]{4,3,2,1,0:T(8,128)}, f32[3,4,4,32,512]{4,3,2,1,0:T(8,128)S(1)}, u32[]{:S(2)}) copy-start(f32[3,4,4,32,512]{4,3,2,1,0:T(8,128)S(1)} %get-tuple-element.17) | copy-start | bytes 9437188
  319.4 5.6 %copy-start.20 = (f32[512,512]{1,0:T(8,128)}, f32[512,512]{1,0:T(8,128)S(1)}, u32[]{:S(2)}) copy-start(f32[512,512]{1,0:T(8,128)S(1)} %fusion.20) | copy-start | bytes 3145732
  319.4 4.1 copy-start.6
  323.4 7.3 %copy-start.8 = (f32[512,512]{0,1:T(8,128)}, f32[512,512]{0,1:T(8,128)S(1)}, u32[]{:S(2)}) copy-start(f32[512,512]{0,1:T(8,128)S(1)} %fusion.39) | copy-start | bytes 3145732
  323.5 2.0 copy-start.14
  328.6 4.7 copy-start.16
  341.6 1.9 copy-start.9
  341.6 2.2 copy-start.15
  341.6 4.4 copy-start.13
  343.4 3.6 copy-start.21
  346.0 2.1 copy-start.27
  347.0 2.1 copy-start.23
  348.1 2.1 copy-start.18
  353.3 5.5 %copy-start.19 = (f32[512,512]{0,1:T(8,128)S(1)}, f32[512,512]{0,1:T(8,128)}, u32[]{:S(2)}) copy-start(f32[512,512]{0,1:T(8,128)} %copy-done.18) | copy-start | bytes 3145732
  356.0 4.2 copy-start.17
  356.0 5.5 %copy-start.10 = (f32[512,512]{0,1:T(8,128)S(1)}, f32[512,512]{0,1:T(8,128)}, u32[]{:S(2)}) copy-start(f32[512,512]{0,1:T(8,128)} %copy-done.8) | copy-start | bytes 3145732
  365.2 95.9 %copy-start.1 = (f32[2,2,4,32,1536]{4,3,2,1,0:T(8,128)S(1)}, f32[2,2,4,32,1536]{4,3,2,1,0:T(8,128)}, u32[]{:S(2)}) copy-start(f32[2,2,4,32,1536]{4,3,2,1,0:T(8,128)} %copy-done) | copy-start | bytes 9437188
  (5 other events, 7.4 us)
